TPU v7x, 512 devices: a whole 4x4x16 slice. The times are simulated.
512 devices in a mesh: mem: 16 (over z_lo, core), lat: 32 (over x, y, z_hi).
Axes of the slice: x: 4, y: 4, z: 16 (z_hi: 2, z_lo: 8; z = z_hi * 8 + z_lo), core: 2. Of those that a mesh axis runs over, the one named last changes fastest.
Arguments:
- control: bfloat16 [32, 10, 704, 1440], P('mem', None, 'lat'), may hold values from -6 to 6
- perturb: bfloat16 [32, 10, 704, 1440], P('mem', None, None, 'lat'), may hold values from -6 to 6
- lon_loc: bfloat16 [1440, 1440], P(None, 'mem'), may hold values from 0 to 1, as said below
- lat_loc: bfloat16 [704, 704], P('mem'), may hold values from 0 to 1, as said below
- static_scale: float32 [10, 704, 1440], P(None, 'mem', 'lat'), may hold values from 0.3 to 1
- static_field: float32 [10, 704, 1440], P(None, 'mem', 'lat'), may hold values from -6 to 6
- courant: float32 [2, 704, 1440], P(None, 'mem', 'lat'), may hold values from -0.48 to 0.48
Outputs:
- increment: float32 [10, 704, 1440], P(None, 'mem', 'lat')
- evolved: float32 [10, 704, 1440], P(None, 'mem', 'lat')
Inputs may be any that keep to these rules, and one draw needn't show every extreme that they name: `lon_loc`: Symmetric, with positive entries. `lat_loc`: Symmetric, with positive entries.
All inputs are finite; a program needn't handle non-finite values.
Results may differ from a plain program's by a relative error of at most 0.0027.
Values may be sent and summed in bfloat16 or wider, within the bound.
A program may use at most 64 MiB of HBM per device.

v0:
```python
import math
import jax
import jax.numpy as jnp
from jax import lax
from jax.sharding import PartitionSpec as P

NLAT = 704
STEPS = 4


def padded_2(shard, sides, width, wrap):
    for axis, dim in sides:
        size, length = (lax.axis_size(axis), shard.shape[dim])
        up = [(i, (i + 1) % size) for i in range(size if wrap else size - 1)]
        down = [(j, i) for i, j in up]
        last = lax.slice_in_dim(shard, length - width, length, axis=dim)
        leading = lax.slice_in_dim(shard, 0, width, axis=dim)
        before = lax.ppermute(last, axis, up)
        after = lax.ppermute(leading, axis, down)
        shard = jnp.concatenate([before, shard, after], axis=dim)
    return shard


def in_order(parts, dim):
    shape = list(parts.shape[1:])
    shape[dim] *= parts.shape[0]
    return jnp.moveaxis(parts, 0, dim).reshape(shape)


def sent_to_all(shard, axis):
    length = lax.axis_size(axis)
    return lax.all_to_all(
        jnp.broadcast_to(shard[None], (length, *shard.shape)), axis, 0, 0, tiled=True
    )


def collect(shard, axis, dim):
    return in_order(sent_to_all(shard, axis), dim)


def upwind(padded, east_west, north_south):
    center = padded[:, 1:-1, 1:-1]
    western = padded[:, 1:-1, :-2]
    eastern = padded[:, 1:-1, 2:]
    southern = padded[:, :-2, 1:-1]
    northern = padded[:, 2:, 1:-1]
    zonal = jnp.maximum(east_west, 0.0) * (center - western) + jnp.minimum(east_west, 0.0) * (
        eastern - center
    )
    meridional = jnp.maximum(north_south, 0.0) * (center - southern) + jnp.minimum(
        north_south, 0.0
    ) * (northern - center)
    return center - zonal - meridional


def lon_rim(values, width):
    return padded_2(values, (("lat", 2),), width, True)


def lat_rim(values, width):
    return padded_2(values, (("mem", 1),), width, False)


def evolve(current, courant):
    fields = current.shape[0]
    stacked = jnp.concatenate([current, courant], axis=0)
    extended = lat_rim(lon_rim(stacked, STEPS), STEPS)
    result = extended[:fields]
    wind_ext = extended[fields:]
    for step_index in range(STEPS):
        margin = step_index + 1
        inner_wind = wind_ext[
            :, margin : wind_ext.shape[1] - margin, margin : wind_ext.shape[2] - margin
        ]
        result = upwind(result, inner_wind[0], inner_wind[1])
    return result


def per_device(control, perturb, lon_loc, lat_loc, static_scale, static_field, courant):
    along_lon = jnp.einsum(
        "mfal,lc->amfc",
        control,
        lax.all_gather(lon_loc, "mem", axis=1, tiled=True),
        preferred_element_type=jnp.float32,
    ).astype(jnp.bfloat16)
    banded = lax.all_to_all(along_lon, "lat", split_axis=3, concat_axis=0, tiled=True)
    mem_here = banded.shape[1]
    fields = banded.shape[2]
    lon_width = banded.shape[3]
    flat_band = banded.reshape(banded.shape[0], mem_here * fields * lon_width)
    pert_rows = jnp.transpose(perturb, (2, 0, 1, 3))
    lat_weights_all = collect(lat_loc, "mem", 0)
    members = mem_here * lax.axis_size("mem")
    ens_scale = 1.0 / math.sqrt(members - 1)
    rows_own = NLAT // lax.axis_size("mem")
    localized = jnp.dot(lat_weights_all, flat_band, preferred_element_type=jnp.float32)
    localized = localized.reshape(NLAT, mem_here, fields, lon_width)
    ensemble_all = jnp.transpose(
        lax.psum(jnp.sum(localized * pert_rows.astype(jnp.float32), axis=1) * ens_scale, "mem"),
        (1, 0, 2),
    )
    offset = lax.axis_index("mem") * rows_own
    ensemble = lax.dynamic_slice_in_dim(ensemble_all, offset, rows_own, 1)
    increment = ensemble + static_scale * static_field
    evolved = evolve(increment, courant)
    return (increment, evolved)


def solution(mesh):
    placed = (
        P("mem", None, "lat", None),
        P("mem", None, None, "lat"),
        P(None, "mem"),
        P("mem", None),
        P(None, "mem", "lat"),
        P(None, "mem", "lat"),
        P(None, "mem", "lat"),
    )
    return jax.shard_map(
        per_device,
        mesh=mesh,
        in_specs=placed,
        out_specs=(P(None, "mem", "lat"), P(None, "mem", "lat")),
        check_vma=False,
    )
```

profile of v0, /device:TPU:1, one launch (start us, length us, event | category | flops | bytes accessed | tf_op | source)
XLA Modules:
  0.0 541.9 jit_solution(11255603198932027136)
XLA Ops:
  7.9 2.0 broadcast_in_dim.2
  9.9 14.0 %all-to-all-start.1 = ((bf16[16,44,704]{2,1,0:T(8,128)(2,1)}), bf16[16,44,704]{2,1,0:T(8,128)(2,1)S(1)}, u32[]{:S(2)}, u32[]{:S(2)}) async-start(bf16[16,44,704]{2,1,0:T(8,128)(2,1)} %broadcast_in_dim.2), calls=%async_computation.1 | async-start | bytes 2359296 | tf_op jit(solution)/shard_map/all_to_all | solution.py:32
  23.9 111.8 %all-gather.3.cloned.1.call-done = bf16[16,90,1440]{2,1,0:T(8,128)(2,1)} async-done(((bf16[1,90,1440]{2,1,0:T(8,128)(2,1)}), bf16[16,90,1440]{2,1,0:T(8,128)(2,1)}) %all-gather.3.cloned.1.call-update) | async-done | bytes 4147216 | tf_op jit(solution)/shard_map/all_gather | solution.py:83
  135.8 5.9 %reshape.20 = bf16[1440,1440,1,1]{1,0,2,3:T(8,128)(2,1)} reshape(bf16[16,90,1440]{2,1,0:T(8,128)(2,1)} %all-gather.3.cloned.1.call-done) | data formatting | bytes 8294400
  141.7 6.0 %fusion.6 = bf16[22,2,10,1440]{3,0,2,1:T(8,128)(2,1)} fusion(bf16[1440,1440,1,1]{1,0,2,3:T(8,128)(2,1)} %reshape.20, bf16[2,10,22,1440]{3,0,2,1:T(2,128)(2,1)S(1)} %copy-done), kind=kOutput, calls=%fused_computation.5 | convolution fusion | flops 1825401600 | bytes 6681600 | tf_op jit(solution)/shard_map/mfal,lc->amfc/dot_general | solution.py:80
  147.7 15.6 %copy.36 = bf16[22,2,10,1440]{0,1,2,3:T(2,128)(2,1)} copy(bf16[22,2,10,1440]{3,0,2,1:T(8,128)(2,1)} %fusion.6) | data formatting | bytes 2534400 | tf_op jit(solution)/shard_map/convert_element_type | solution.py:85
  163.3 11.0 %reshape.22 = bf16[32,2,9900]{2,1,0:T(2,128)(2,1)} reshape(bf16[1440,10,2,22]{3,2,1,0:T(2,128)(2,1)} %bitcast.62) | data formatting | bytes 2534400
  175.3 12.5 %all-to-all-start = ((bf16[32,2,9900]{2,1,0:T(2,128)(2,1)}), bf16[32,2,9900]{2,1,0:T(2,128)(2,1)S(1)}, u32[]{:S(2)}, u32[]{:S(2)}) async-start(bf16[32,2,9900]{2,1,0:T(2,128)(2,1)} %reshape.22), calls=%async_computation | async-start | bytes 2555904 | tf_op jit(solution)/shard_map/all_to_all | solution.py:86
  187.9 2.3 reshape.16
  190.2 44.9 %all-to-all-done = bf16[32,2,9900]{2,1,0:T(2,128)(2,1)S(1)} async-done(((bf16[32,2,9900]{2,1,0:T(2,128)(2,1)}), bf16[32,2,9900]{2,1,0:T(2,128)(2,1)S(1)}, u32[]{:S(2)}, u32[]{:S(2)}) %all-to-all-start) | async-done | bytes 1267232 | tf_op jit(solution)/shard_map/all_to_all | solution.py:86
  235.1 7.4 %reshape.23 = bf16[1440,10,2,22]{3,2,1,0:T(2,128)(2,1)} reshape(bf16[32,2,9900]{2,1,0:T(2,128)(2,1)S(1)} %all-to-all-done) | data formatting | bytes 2534400
  242.5 25.1 %copy.53 = bf16[22,2,10,32,45]{4,2,1,0,3:T(8,128)(2,1)} copy(bf16[22,2,10,32,45]{0,1,2,4,3:T(2,128)(2,1)} %bitcast.61) | data formatting | bytes 2534400 | tf_op jit(solution)/shard_map/all_to_all | solution.py:86
  267.6 7.9 %reshape.15 = bf16[704,900]{1,0:T(8,128)(2,1)S(1)} reshape(bf16[32,22,2,10,45]{4,3,2,1,0:T(8,128)(2,1)} %bitcast.63) | data formatting | bytes 2534400 | tf_op jit(solution)/shard_map/reshape | solution.py:90
  275.5 4.3 convolution_bitcast_fusion
  279.8 3.9 reshape.17
  283.7 2.5 fusion.2
  286.2 1.2 broadcast_multiply_fusion
  288.9 206.1 %all-reduce.2.cloned.1.call-done = f32[704,10,45]{0,2,1:T(8,128)} async-done(((f32[704,10,45]{0,2,1:T(8,128)}), f32[704,10,45]{0,2,1:T(8,128)}) %all-reduce.2.cloned.1.call-update) | async-done | bytes 1267216 | tf_op jit(solution)/shard_map/psum | solution.py:99
  495.0 1.2 bitcast_add_fusion
  496.2 8.1 %collective-permute-start = (f32[12,44,4]{1,2,0:T(4,128)S(1)}, f32[12,44,4]{1,2,0:T(4,128)S(1)}, u32[]{:S(2)}, u32[]{:S(2)}) collective-permute-start(f32[12,44,4]{1,2,0:T(4,128)S(1)} %get-tuple-element.26), channel_id=1, source_target_pairs={{0,1},{1,2},{2,3},{3,4},{4,5},{5,6},{6,7},{7,8},{8,9},{9,10},{10,1... | collective-permute-start | bytes 25352 | tf_op jit(solution)/shard_map/ppermute | solution.py:18
  504.4 10.1 %collective-permute-start.1 = (f32[12,44,4]{1,2,0:T(4,128)S(1)}, f32[12,44,4]{1,2,0:T(4,128)S(1)}, u32[]{:S(2)}, u32[]{:S(2)}) collective-permute-start(f32[12,44,4]{1,2,0:T(4,128)S(1)} %get-tuple-element.27), channel_id=1, source_target_pairs={{1,0},{2,1},{3,2},{4,3},{5,4},{6,5},{7,6},{8,7},{9,8},{10,9},{11,1... | collective-permute-start | bytes 25352 | tf_op jit(solution)/shard_map/ppermute | solution.py:19
  514.5 3.4 collective-permute-done.1
  518.2 4.9 collective-permute-start.2
  523.1 7.6 %collective-permute-start.3 = (f32[12,4,53]{1,2,0:T(8,128)S(1)}, f32[12,4,53]{1,2,0:T(8,128)S(1)}, u32[]{:S(2)}, u32[]{:S(2)}) collective-permute-start(f32[12,4,53]{1,2,0:T(8,128)S(1)} %get-tuple-element.25), channel_id=1, source_target_pairs={{32,0},{64,32},{96,64},{128,96},{160,128},{192,160},{224,192},{256... | collective-permute-start | bytes 30536 | tf_op jit(solution)/shard_map/ppermute | solution.py:19
  (45 shorter events, 7.6 us)
Async XLA Ops:
  7.2 134.5 %copy-start = (bf16[2,10,22,1440]{3,0,2,1:T(2,128)(2,1)S(1)}, bf16[2,10,22,1440]{3,0,2,1:T(2,128)(2,1)}, u32[]{:S(2)}) copy-start(bf16[2,10,22,1440]{3,0,2,1:T(2,128)(2,1)} %param.7) | copy-start | bytes 3801604
  7.2 128.6 %all-gather.3.cloned.1.call-start = ((), (), s32[]{:S(2)}) async-start(), calls=%async_computation.3 | async-start | bytes 5013504 | tf_op jit(solution)/shard_map/all_gather | solution.py:83
  9.9 164.4 %all-to-all-start.1 = ((bf16[16,44,704]{2,1,0:T(8,128)(2,1)}), bf16[16,44,704]{2,1,0:T(8,128)(2,1)S(1)}, u32[]{:S(2)}, u32[]{:S(2)}) async-start(bf16[16,44,704]{2,1,0:T(8,128)(2,1)} %broadcast_in_dim.2), calls=%async_computation.1 | async-start | bytes 2359296 | tf_op jit(solution)/shard_map/all_to_all | solution.py:32
  174.3 1.0 copy-start.1
  175.3 59.7 %all-to-all-start = ((bf16[32,2,9900]{2,1,0:T(2,128)(2,1)}), bf16[32,2,9900]{2,1,0:T(2,128)(2,1)S(1)}, u32[]{:S(2)}, u32[]{:S(2)}) async-start(bf16[32,2,9900]{2,1,0:T(2,128)(2,1)} %reshape.22), calls=%async_computation | async-start | bytes 2555904 | tf_op jit(solution)/shard_map/all_to_all | solution.py:86
  187.8 307.2 %all-reduce.2.cloned.1.call-start = ((), (), s32[]{:S(2)}) async-start(), calls=%async_computation.2 | async-start | bytes 2949120 | tf_op jit(solution)/shard_map/psum | solution.py:99
  279.8 3.9 copy-start.2
  287.5 0.9 copy-start.3
  287.5 1.1 copy-start.4
  287.5 1.3 copy-start.5
  496.2 18.3 %collective-permute-start = (f32[12,44,4]{1,2,0:T(4,128)S(1)}, f32[12,44,4]{1,2,0:T(4,128)S(1)}, u32[]{:S(2)}, u32[]{:S(2)}) collective-permute-start(f32[12,44,4]{1,2,0:T(4,128)S(1)} %get-tuple-element.26), channel_id=1, source_target_pairs={{0,1},{1,2},{2,3},{3,4},{4,5},{5,6},{6,7},{7,8},{8,9},{9,10},{10,1... | collective-permute-start | bytes 25352 | tf_op jit(solution)/shard_map/ppermute | solution.py:18
  504.4 13.6 %collective-permute-start.1 = (f32[12,44,4]{1,2,0:T(4,128)S(1)}, f32[12,44,4]{1,2,0:T(4,128)S(1)}, u32[]{:S(2)}, u32[]{:S(2)}) collective-permute-start(f32[12,44,4]{1,2,0:T(4,128)S(1)} %get-tuple-element.27), channel_id=1, source_target_pairs={{1,0},{2,1},{3,2},{4,3},{5,4},{6,5},{7,6},{8,7},{9,8},{10,9},{11,1... | collective-permute-start | bytes 25352 | tf_op jit(solution)/shard_map/ppermute | solution.py:19
  518.2 13.9 %collective-permute-start.2 = (f32[12,4,53]{1,2,0:T(8,128)S(1)}, f32[12,4,53]{1,2,0:T(8,128)S(1)}, u32[]{:S(2)}, u32[]{:S(2)}) collective-permute-start(f32[12,4,53]{1,2,0:T(8,128)S(1)} %get-tuple-element.24), channel_id=1, source_target_pairs={{0,32},{32,64},{64,96},{96,128},{128,160},{160,192},{192,224},{224... | collective-permute-start | bytes 30536 | tf_op jit(solution)/shard_map/ppermute | solution.py:18
  523.1 8.9 %collective-permute-start.3 = (f32[12,4,53]{1,2,0:T(8,128)S(1)}, f32[12,4,53]{1,2,0:T(8,128)S(1)}, u32[]{:S(2)}, u32[]{:S(2)}) collective-permute-start(f32[12,4,53]{1,2,0:T(8,128)S(1)} %get-tuple-element.25), channel_id=1, source_target_pairs={{32,0},{64,32},{96,64},{128,96},{160,128},{192,160},{224,192},{256... | collective-permute-start | bytes 30536 | tf_op jit(solution)/shard_map/ppermute | solution.py:19
Sparse Core Ops, SparseCore 0:
  10.1 125.6 all-gather.2
  287.6 207.3 all-reduce.1
where the time goes:
time: 545 us; the launch traced here: 542 us
  waiting for transfers between devices  367 us (67%)
  local copies, waits for them, and re-layouts  86 us (16%)
  starting transfers between devices  57.4 us (11%)
  between operations  14.2 us (3%)
  matrix products  10.2 us (2%)
  other arithmetic  7.06 us (1%)
    psum x1, waiting for transfers between devices, per_device(): lax.psum(jnp.sum(localized * pert_rows.astype(jnp.float32), axis=1) * ens...  206 us
    all_gather x1, waiting for transfers between devices, per_device(): lax.all_gather(lon_loc, 'mem', axis=1, tiled=True)  112 us
    all_to_all x1, waiting for transfers between devices, per_device(): lax.all_to_all(along_lon, 'lat', split_axis=3, concat_axis=0, tiled=True)  44.9 us
    unnamed x20, local copies, waits for them, and re-layouts  28.6 us
    all_to_all x1, local copies, waits for them, and re-layouts, per_device(): lax.all_to_all(along_lon, 'lat', split_axis=3, concat_axis=0, tiled=True)  25.1 us
    ppermute x2, starting transfers between devices, padded_2(): after = lax.ppermute(leading, axis, down)  17.7 us
    convert_element_type x1, local copies, waits for them, and re-layouts, per_device(): along_lon = jnp.einsum('mfal,lc->amfc', control, lax.all_gather(lon_loc,...  15.6 us
    all_to_all x1, starting transfers between devices, sent_to_all(): lax.all_to_all(jnp.broadcast_to(shard[None], (length, *shard.shape)), axi...  14 us
  transfers between devices with their start and end apart: 8, of which 4 were waited for; matrix products, arithmetic and copies ran while one was open for 8% of the time, Pallas kernels for 0%

commit v1 on v0

--- a/solution.py
+++ b/solution.py
@@ -80,7 +80,9 @@
     along_lon = jnp.einsum(
         "mfal,lc->amfc",
         control,
-        lax.all_gather(lon_loc, "mem", axis=1, tiled=True),
+        jnp.concatenate(
+            lax.all_to_all(jnp.stack([lon_loc] * lax.axis_size("mem")), "mem", 0, 0), axis=1
+        ),
         preferred_element_type=jnp.float32,
     ).astype(jnp.bfloat16)
     banded = lax.all_to_all(along_lon, "lat", split_axis=3, concat_axis=0, tiled=True)

time: 545 us -> 666 us (1.22)
  blocking collectives: 0 us -> 221 us
  waiting for transfers between devices: 367 us -> 274 us
  starting transfers between devices: 57.4 us -> 49.9 us
    all_to_all x0 -> x1, blocking collectives: none -> 221 us  [per_device(): lax.all_to_all(jnp.stack([lon_loc] * lax.axis_size('mem')), 'mem', 0, 0)]
    all_gather x1 -> x0, waiting for transfers between devices: 112 us -> none  [per_device(): lax.all_gather(lon_loc, 'mem', axis=1, tiled=True)]
    psum x1, waiting for transfers between devices: 206 us -> 233 us  [per_device(): lax.psum(jnp.sum(localized * pert_rows.astype(jnp.float32), axis=1) * ens...]
    all_to_all x1, waiting for transfers between devices: 44.9 us -> 27.3 us  [per_device(): lax.all_to_all(along_lon, 'lat', split_axis=3, concat_axis=0, tiled=True)]
    all_to_all x1, waiting for transfers between devices: 0.01 us -> 10.5 us  [sent_to_all(): lax.all_to_all(jnp.broadcast_to(shard[None], (length, *shard.shape)), axi...]
    all_to_all x1, starting transfers between devices: 14 us -> 6.27 us  [sent_to_all(): lax.all_to_all(jnp.broadcast_to(shard[None], (length, *shard.shape)), axi...]
    unnamed x20 -> x21, local copies, waits for them, and re-layouts: 28.6 us -> 22.7 us
  transfers between devices with their start and end apart: 8 -> 7, of which waited for: 4 -> 4; matrix products, arithmetic and copies ran while one was open for 8% -> 6% of each run, Pallas kernels for 0% -> 0%
where the time goes in v1:
time: 666 us; the launch traced here: 663 us
  waiting for transfers between devices  274 us (41%)
  blocking collectives  221 us (33%)
  local copies, waits for them, and re-layouts  86.6 us (13%)
  starting transfers between devices  49.9 us (7%)
  between operations  14.3 us (2%)
  matrix products  10.2 us (2%)
  other arithmetic  7.07 us (1%)
    psum x1, waiting for transfers between devices, per_device(): lax.psum(jnp.sum(localized * pert_rows.astype(jnp.float32), axis=1) * ens...  233 us
    all_to_all x1, blocking collectives, per_device(): lax.all_to_all(jnp.stack([lon_loc] * lax.axis_size('mem')), 'mem', 0, 0)  221 us
    all_to_all x1, waiting for transfers between devices, per_device(): lax.all_to_all(along_lon, 'lat', split_axis=3, concat_axis=0, tiled=True)  27.3 us
    all_to_all x1, local copies, waits for them, and re-layouts, per_device(): lax.all_to_all(along_lon, 'lat', split_axis=3, concat_axis=0, tiled=True)  25.1 us
    unnamed x21, local copies, waits for them, and re-layouts  22.7 us
    ppermute x2, starting transfers between devices, padded_2(): after = lax.ppermute(leading, axis, down)  17.7 us
    convert_element_type x1, local copies, waits for them, and re-layouts, per_device(): along_lon = jnp.einsum('mfal,lc->amfc', control, jnp.concatenate(lax.all_...  15.6 us
  transfers between devices with their start and end apart: 7, of which 4 were waited for; matrix products, arithmetic and copies ran while one was open for 6% of the time, Pallas kernels for 0%

profile of v1, /device:TPU:1, one launch (start us, length us, event | category | flops | bytes accessed | tf_op | source)
XLA Modules:
  0.0 663.2 jit_solution(14590434603605455101)
XLA Ops:
  7.2 1.5 stack.2
  8.7 221.2 %all_to_all.25 = bf16[16,1440,90]{1,2,0:T(8,128)(2,1)} all-to-all(bf16[16,1440,90]{1,2,0:T(8,128)(2,1)S(1)} %stack.2), channel_id=1, replica_groups=mesh['mem'=16,'lat'=32] {'mem'}, dimensions={0} | all-to-all | bytes 8294400 | tf_op jit(solution)/shard_map/all_to_all | solution.py:84
  231.0 6.3 all-to-all-start.2
  237.3 5.9 reshape.24
  243.2 5.9 fusion.6
  249.2 15.6 %copy.40 = bf16[22,2,10,1440]{0,1,2,3:T(2,128)(2,1)} copy(bf16[22,2,10,1440]{3,0,2,1:T(8,128)(2,1)} %fusion.6) | data formatting | bytes 2534400 | tf_op jit(solution)/shard_map/convert_element_type | solution.py:87
  264.8 11.1 %reshape.29 = bf16[32,2,9900]{2,1,0:T(2,128)(2,1)} reshape(bf16[1440,10,2,22]{3,2,1,0:T(2,128)(2,1)} %bitcast.62) | data formatting | bytes 2534400
  275.9 10.5 %all-to-all-done.2 = bf16[16,44,704]{2,1,0:T(8,128)(2,1)S(1)} async-done(((bf16[16,44,704]{2,1,0:T(8,128)(2,1)}), bf16[16,44,704]{2,1,0:T(8,128)(2,1)S(1)}, u32[]{:S(2)}, u32[]{:S(2)}) %all-to-all-start.2) | async-done | bytes 991264 | tf_op jit(solution)/shard_map/all_to_all | solution.py:32
  287.4 12.8 %all-to-all-start.1 = ((bf16[32,2,9900]{2,1,0:T(2,128)(2,1)}), bf16[32,2,9900]{2,1,0:T(2,128)(2,1)S(1)}, u32[]{:S(2)}, u32[]{:S(2)}) async-start(bf16[32,2,9900]{2,1,0:T(2,128)(2,1)} %reshape.29), calls=%async_computation.1 | async-start | bytes 2555904 | tf_op jit(solution)/shard_map/all_to_all | solution.py:88
  300.2 2.3 reshape.26
  302.5 27.3 %all-to-all-done.1 = bf16[32,2,9900]{2,1,0:T(2,128)(2,1)S(1)} async-done(((bf16[32,2,9900]{2,1,0:T(2,128)(2,1)}), bf16[32,2,9900]{2,1,0:T(2,128)(2,1)S(1)}, u32[]{:S(2)}, u32[]{:S(2)}) %all-to-all-start.1) | async-done | bytes 1267232 | tf_op jit(solution)/shard_map/all_to_all | solution.py:88
  329.8 7.4 %reshape.30 = bf16[1440,10,2,22]{3,2,1,0:T(2,128)(2,1)} reshape(bf16[32,2,9900]{2,1,0:T(2,128)(2,1)S(1)} %all-to-all-done.1) | data formatting | bytes 2534400
  337.2 25.1 %copy.58 = bf16[22,2,10,32,45]{4,2,1,0,3:T(8,128)(2,1)} copy(bf16[22,2,10,32,45]{0,1,2,4,3:T(2,128)(2,1)} %bitcast.61) | data formatting | bytes 2534400 | tf_op jit(solution)/shard_map/all_to_all | solution.py:88
  362.3 7.9 %reshape.25 = bf16[704,900]{1,0:T(8,128)(2,1)S(1)} reshape(bf16[32,22,2,10,45]{4,3,2,1,0:T(8,128)(2,1)} %bitcast.63) | data formatting | bytes 2534400 | tf_op jit(solution)/shard_map/reshape | solution.py:92
  370.2 4.3 convolution_bitcast_fusion
  374.5 3.9 reshape.27
  378.4 2.5 fusion.2
  381.0 1.3 broadcast_multiply_fusion
  383.6 232.7 %all-reduce.2.cloned.1.call-done = f32[704,10,45]{0,2,1:T(8,128)} async-done(((f32[704,10,45]{0,2,1:T(8,128)}), f32[704,10,45]{0,2,1:T(8,128)}) %all-reduce.2.cloned.1.call-update) | async-done | bytes 1267216 | tf_op jit(solution)/shard_map/psum | solution.py:101
  617.6 8.1 %collective-permute-start = (f32[12,44,4]{1,2,0:T(4,128)S(1)}, f32[12,44,4]{1,2,0:T(4,128)S(1)}, u32[]{:S(2)}, u32[]{:S(2)}) collective-permute-start(f32[12,44,4]{1,2,0:T(4,128)S(1)} %get-tuple-element.26), channel_id=1, source_target_pairs={{0,1},{1,2},{2,3},{3,4},{4,5},{5,6},{6,7},{7,8},{8,9},{9,10},{10,1... | collective-permute-start | bytes 25352 | tf_op jit(solution)/shard_map/ppermute | solution.py:18
  625.7 10.1 %collective-permute-start.1 = (f32[12,44,4]{1,2,0:T(4,128)S(1)}, f32[12,44,4]{1,2,0:T(4,128)S(1)}, u32[]{:S(2)}, u32[]{:S(2)}) collective-permute-start(f32[12,44,4]{1,2,0:T(4,128)S(1)} %get-tuple-element.27), channel_id=1, source_target_pairs={{1,0},{2,1},{3,2},{4,3},{5,4},{6,5},{7,6},{8,7},{9,8},{10,9},{11,1... | collective-permute-start | bytes 25352 | tf_op jit(solution)/shard_map/ppermute | solution.py:19
  635.8 3.4 collective-permute-done.1
  639.5 4.9 collective-permute-start.2
  644.4 7.6 %collective-permute-start.3 = (f32[12,4,53]{1,2,0:T(8,128)S(1)}, f32[12,4,53]{1,2,0:T(8,128)S(1)}, u32[]{:S(2)}, u32[]{:S(2)}) collective-permute-start(f32[12,4,53]{1,2,0:T(8,128)S(1)} %get-tuple-element.25), channel_id=1, source_target_pairs={{32,0},{64,32},{96,64},{128,96},{160,128},{192,160},{224,192},{256... | collective-permute-start | bytes 30536 | tf_op jit(solution)/shard_map/ppermute | solution.py:19
  (46 shorter events, 9.2 us)
Async XLA Ops:
  7.2 236.1 %copy-start = (bf16[2,10,22,1440]{3,0,2,1:T(2,128)(2,1)S(1)}, bf16[2,10,22,1440]{3,0,2,1:T(2,128)(2,1)}, u32[]{:S(2)}) copy-start(bf16[2,10,22,1440]{3,0,2,1:T(2,128)(2,1)} %param.7) | copy-start | bytes 3801604
  8.7 221.2 %copy-start.6 = (bf16[44,704]{1,0:T(8,128)(2,1)S(1)}, bf16[44,704]{1,0:T(8,128)(2,1)}, u32[]{:S(2)}) copy-start(bf16[44,704]{1,0:T(8,128)(2,1)} %param.10) | copy-start | bytes 185860
  231.0 55.3 %all-to-all-start.2 = ((bf16[16,44,704]{2,1,0:T(8,128)(2,1)}), bf16[16,44,704]{2,1,0:T(8,128)(2,1)S(1)}, u32[]{:S(2)}, u32[]{:S(2)}) async-start(bf16[16,44,704]{2,1,0:T(8,128)(2,1)} %broadcast_in_dim.2), calls=%async_computation.2 | async-start | bytes 2359296 | tf_op jit(solution)/shard_map/all_to_all | solution.py:32
  286.4 1.0 copy-start.1
  287.4 42.4 %all-to-all-start.1 = ((bf16[32,2,9900]{2,1,0:T(2,128)(2,1)}), bf16[32,2,9900]{2,1,0:T(2,128)(2,1)S(1)}, u32[]{:S(2)}, u32[]{:S(2)}) async-start(bf16[32,2,9900]{2,1,0:T(2,128)(2,1)} %reshape.29), calls=%async_computation.1 | async-start | bytes 2555904 | tf_op jit(solution)/shard_map/all_to_all | solution.py:88
  300.2 316.2 %all-reduce.2.cloned.1.call-start = ((), (), s32[]{:S(2)}) async-start(), calls=%async_computation.3 | async-start | bytes 2949120 | tf_op jit(solution)/shard_map/psum | solution.py:101
  374.5 3.9 copy-start.2
  382.2 0.9 copy-start.3
  382.2 1.1 copy-start.4
  382.2 1.3 copy-start.5
  617.6 18.3 %collective-permute-start = (f32[12,44,4]{1,2,0:T(4,128)S(1)}, f32[12,44,4]{1,2,0:T(4,128)S(1)}, u32[]{:S(2)}, u32[]{:S(2)}) collective-permute-start(f32[12,44,4]{1,2,0:T(4,128)S(1)} %get-tuple-element.26), channel_id=1, source_target_pairs={{0,1},{1,2},{2,3},{3,4},{4,5},{5,6},{6,7},{7,8},{8,9},{9,10},{10,1... | collective-permute-start | bytes 25352 | tf_op jit(solution)/shard_map/ppermute | solution.py:18
  625.7 13.6 %collective-permute-start.1 = (f32[12,44,4]{1,2,0:T(4,128)S(1)}, f32[12,44,4]{1,2,0:T(4,128)S(1)}, u32[]{:S(2)}, u32[]{:S(2)}) collective-permute-start(f32[12,44,4]{1,2,0:T(4,128)S(1)} %get-tuple-element.27), channel_id=1, source_target_pairs={{1,0},{2,1},{3,2},{4,3},{5,4},{6,5},{7,6},{8,7},{9,8},{10,9},{11,1... | collective-permute-start | bytes 25352 | tf_op jit(solution)/shard_map/ppermute | solution.py:19
  639.5 13.9 %collective-permute-start.2 = (f32[12,4,53]{1,2,0:T(8,128)S(1)}, f32[12,4,53]{1,2,0:T(8,128)S(1)}, u32[]{:S(2)}, u32[]{:S(2)}) collective-permute-start(f32[12,4,53]{1,2,0:T(8,128)S(1)} %get-tuple-element.24), channel_id=1, source_target_pairs={{0,32},{32,64},{64,96},{96,128},{128,160},{160,192},{192,224},{224... | collective-permute-start | bytes 30536 | tf_op jit(solution)/shard_map/ppermute | solution.py:18
  644.4 8.9 %collective-permute-start.3 = (f32[12,4,53]{1,2,0:T(8,128)S(1)}, f32[12,4,53]{1,2,0:T(8,128)S(1)}, u32[]{:S(2)}, u32[]{:S(2)}) collective-permute-start(f32[12,4,53]{1,2,0:T(8,128)S(1)} %get-tuple-element.25), channel_id=1, source_target_pairs={{32,0},{64,32},{96,64},{128,96},{160,128},{192,160},{224,192},{256... | collective-permute-start | bytes 30536 | tf_op jit(solution)/shard_map/ppermute | solution.py:19
Sparse Core Ops, SparseCore 0:
  382.4 233.9 all-reduce.1
